TPU v7x, 32 devices: a whole 2x2x4 slice. The times are simulated.
32 devices in a mesh: section: 8 (over z, core), tensor: 4 (over y, x).
Axes of the slice: x: 2, y: 2, z: 4, core: 2. Of those that a mesh axis runs over, the one named last changes fastest.
Arguments:
- fwd_in: bfloat16 [8, 128, 2304], P('section', None, 'tensor'), may hold values from -6 to 6
- back_in: bfloat16 [8, 128, 2304], P('section', None, 'tensor'), may hold values from -0.59765625 to 0.59765625
- stash: bfloat16 [2, 8, 128, 2304], P(None, 'section', None, 'tensor'), may hold values from -6 to 6
- w_qkv: bfloat16 [8, 2304, 3, 4, 128], P('section', None, None, 'tensor'), may hold values from -0.125 to 0.125
- w_out: bfloat16 [8, 4, 128, 2304], P('section', 'tensor'), may hold values from -0.25 to 0.25
- norm_gain: bfloat16 [8, 2304], P('section'), may hold values from 0.25 to 1.75
- final_gain: bfloat16 [2304], replicated, may hold values from 0.25 to 1.75
- table: bfloat16 [8192, 2304], P(('section', 'tensor')), may hold values from -0.5625 to 0.5625
- ids: int32 [2, 128], replicated, may hold values from 0 to 8191
- back_ids: int32 [2, 128], replicated, may hold values from 0 to 8191
- targets: int32 [2, 128], replicated, may hold values from 0 to 8191
Outputs:
- fwd_out: bfloat16 [8, 128, 2304], P('section', None, 'tensor')
- back_out: bfloat16 [8, 128, 2304], P('section', None, 'tensor')
- table_grad: bfloat16 [8192, 2304], P(('section', 'tensor'))
- losses: float32 [2], replicated
All inputs are finite; a program needn't handle non-finite values.
Results may differ from a plain program's by a relative error of at most 0.035.
Values may be sent and summed in bfloat16 or wider, within the bound.
No kernel may reach another device: no remote copies, remote signals or barrier semaphores. Data moves between devices by JAX's collectives and lax.ppermute only.
A program may use at most 64 MiB of HBM per device.

v0:
```python
import math
import jax
import jax.numpy as jnp
from jax import lax
from jax.sharding import PartitionSpec as P

EPS = 1e-06
ATTN_CAP = 50.0
LOGIT_CAP = 30.0


def for_sending(x):

    def short(part):
        return part.astype(jnp.bfloat16) if part.dtype == jnp.float32 else part

    return jax.tree.map(short, x)


def passed_along(block, axis, distance):
    devices = range(lax.axis_size(axis))
    route = [(i - distance, i) for i in devices if i - distance in devices]
    return lax.ppermute(block, axis, route)


def broadcast(block, axis, holder):
    block = jnp.where(lax.axis_index(axis) == holder, block, jnp.zeros_like(block))
    return lax.psum(block, axis)


def widen(values):
    return jax.tree.map(
        lambda part, own: part.astype(own.dtype),
        lax.all_gather(for_sending(values), "tensor", axis=1, tiled=True),
        values,
    )


def sum_width(term):
    return lax.psum_scatter(
        term.astype(jnp.bfloat16), "tensor", scatter_dimension=1, tiled=True
    ).astype(jnp.float32)


def stat_width(values):
    return lax.psum(values, "tensor")


def sum_section(values):
    return jax.tree.map(
        lambda part: part.astype(jnp.float32), lax.psum(for_sending(values), "section")
    )


def pass_section(values, offset):
    return passed_along(values, "section", offset)


def feed(values, root):
    return broadcast(widen(values), "section", root)


def reduce_lookup(parts, width_pos, piece):
    summed = lax.psum(parts, ("section", "tensor"))
    return lax.dynamic_slice_in_dim(summed, width_pos * piece, piece, 1)


def row_scale(values):
    return lax.rsqrt(jnp.mean(values * values, axis=-1, keepdims=True) + EPS)


def attend(normed, weights):
    qkv = jnp.einsum("rd,dchk->chrk", normed, weights, preferred_element_type=jnp.float32).astype(
        jnp.bfloat16
    )
    query, keys, values = (qkv[0], qkv[1], qkv[2])
    length = normed.shape[0]
    scores = jnp.einsum(
        "hqk,hsk->hqs", query, keys, preferred_element_type=jnp.float32
    ) * query.shape[-1] ** (-0.5)
    capped = jnp.tanh(scores / ATTN_CAP)
    places = lax.iota(jnp.int32, length)
    causal = places[None, :] <= places[:, None]
    raised = jnp.where(causal[None], jnp.exp(ATTN_CAP * capped), 0.0)
    probs = (raised / jnp.sum(raised, axis=-1, keepdims=True)).astype(jnp.bfloat16)
    mixed = jnp.einsum("hqs,hsk->hqk", probs, values, preferred_element_type=jnp.float32).astype(
        jnp.bfloat16
    )
    return (query, keys, values, capped, probs, mixed)


def norm_back(xfull, xpiece, gpiece, dnorm, full_width):
    scale = row_scale(xfull)
    stat = stat_width(jnp.sum(xpiece * gpiece * dnorm, axis=1))
    return scale * gpiece * dnorm - xpiece * scale**3 * stat[:, None] / full_width


def body(
    fwd_in, back_in, stash, w_qkv, w_out, norm_gain, final_gain, table, ids, back_ids, targets
):
    section_pos = lax.axis_index("section")
    section_count = lax.axis_size("section")
    width_pos = lax.axis_index("tensor")
    width_count = lax.axis_size("tensor")
    acts = fwd_in[0]
    cots = back_in[0]
    rows, piece = acts.shape
    full_width = piece * width_count
    vocab_rows = table.shape[0]
    first_col = (section_pos * width_count + width_pos) * vocab_rows
    columns = first_col + lax.iota(jnp.int32, vocab_rows)
    emb_scale = math.sqrt(full_width)
    gain = norm_gain[0].astype(jnp.float32)
    gain_piece = lax.dynamic_slice_in_dim(gain, width_pos * piece, piece, 0)
    fgain = final_gain.astype(jnp.float32)
    fgain_piece = lax.dynamic_slice_in_dim(fgain, width_pos * piece, piece, 0)
    weights = w_qkv[0]
    outw = w_out[0]
    ticks = ids.shape[0]
    is_first = section_pos == 0
    is_last = section_pos == section_count - 1
    grad = jnp.zeros((vocab_rows, full_width), jnp.float32)
    losses = []
    previous = acts
    for tick in range(ticks):
        xfull = widen(acts).astype(jnp.float32)
        normed = (xfull * row_scale(xfull) * gain).astype(jnp.bfloat16)
        mixed = attend(normed, weights)[5]
        part = jnp.einsum("hrk,hkd->rd", mixed, outw, preferred_element_type=jnp.float32)
        outs_fwd = (acts.astype(jnp.float32) + sum_width(part)).astype(jnp.bfloat16)
        hidden = feed(outs_fwd, section_count - 1).astype(jnp.float32)
        hscale = row_scale(hidden)
        hnormed = (hidden * hscale * fgain).astype(jnp.bfloat16)
        raw = lax.dot_general(
            hnormed, table, (((1,), (1,)), ((), ())), preferred_element_type=jnp.float32
        )
        capped = jnp.tanh(raw / LOGIT_CAP)
        logits = LOGIT_CAP * capped
        raised = jnp.exp(logits)
        hit = targets[tick][:, None] == columns[None, :]
        tile_sums = stat_width(
            (jnp.sum(raised, axis=1), jnp.sum(jnp.where(hit, logits, 0.0), axis=1))
        )
        total, picked = sum_section(tile_sums)
        losses.append(jnp.mean(jnp.log(total) - picked))
        dlog = (
            (raised / total[:, None] - hit.astype(jnp.float32)) * (1.0 - capped * capped)
        ).astype(jnp.bfloat16)
        dpart = jnp.dot(dlog, table, preferred_element_type=jnp.float32)
        dhid = sum_section(sum_width(dpart))
        grad = grad + lax.dot_general(
            dlog, hnormed, (((0,), (0,)), ((), ())), preferred_element_type=jnp.float32
        )
        hpiece = lax.dynamic_slice_in_dim(hidden, width_pos * piece, piece, 1)
        cot_last = norm_back(hidden, hpiece, fgain_piece, dhid, full_width).astype(jnp.bfloat16)
        inputs_back = stash[tick, 0]
        if tick > 0:
            inputs_back = jnp.where(is_last, previous, inputs_back)
        bfull, upper = widen((inputs_back, cots))
        bfloat = bfull.astype(jnp.float32)
        bnormed = (bfloat * row_scale(bfloat) * gain).astype(jnp.bfloat16)
        query, keys, values, acapped, probs, amixed = attend(bnormed, weights)
        dmix = jnp.einsum("rd,hkd->hrk", upper, outw, preferred_element_type=jnp.float32).astype(
            jnp.bfloat16
        )
        dprob = jnp.einsum("hrk,hsk->hrs", dmix, values, preferred_element_type=jnp.float32)
        pfull = probs.astype(jnp.float32)
        dscore = pfull * (dprob - jnp.sum(dprob * pfull, axis=-1, keepdims=True))
        dlogit = (dscore * (1.0 - acapped * acapped) * query.shape[-1] ** (-0.5)).astype(
            jnp.bfloat16
        )
        dquery = jnp.einsum(
            "hqs,hsk->hqk", dlogit, keys, preferred_element_type=jnp.float32
        ).astype(jnp.bfloat16)
        dkeys = jnp.einsum(
            "hqs,hqk->hsk", dlogit, query, preferred_element_type=jnp.float32
        ).astype(jnp.bfloat16)
        dvalues = jnp.einsum(
            "hqs,hqk->hsk", probs, dmix, preferred_element_type=jnp.float32
        ).astype(jnp.bfloat16)
        stacked = jnp.stack([dquery, dkeys, dvalues])
        dterm = jnp.einsum("chrk,dchk->rd", stacked, weights, preferred_element_type=jnp.float32)
        dnorm = sum_width(dterm)
        bpiece = lax.dynamic_slice_in_dim(bfloat, width_pos * piece, piece, 1)
        dxf = norm_back(bfloat, bpiece, gain_piece, dnorm, full_width)
        outs_back = (cots.astype(jnp.float32) + dxf).astype(jnp.bfloat16)
        leaving = feed(outs_back, 0)
        back_hits = (back_ids[tick][:, None] == columns[None, :]).astype(jnp.bfloat16)
        look_grad = lax.dot_general(
            back_hits, leaving, (((0,), (0,)), ((), ())), preferred_element_type=jnp.float32
        )
        grad = grad + look_grad * emb_scale
        hits = (ids[tick][:, None] == columns[None, :]).astype(jnp.bfloat16)
        embedded = reduce_lookup(
            jnp.dot(hits, table, preferred_element_type=jnp.float32), width_pos, piece
        )
        entering = (embedded * emb_scale).astype(jnp.bfloat16)
        previous = acts
        acts = jnp.where(is_first, entering, pass_section(outs_fwd, 1))
        cots = jnp.where(is_last, cot_last, pass_section(outs_back, -1))
    return (acts[None], cots[None], grad.astype(jnp.bfloat16), jnp.stack(losses))


def solution(mesh):
    return jax.shard_map(
        body,
        mesh=mesh,
        in_specs=(
            P("section", None, "tensor"),
            P("section", None, "tensor"),
            P(None, "section", None, "tensor"),
            P("section", None, None, "tensor", None),
            P("section", "tensor", None, None),
            P("section", None),
            P(),
            P(("section", "tensor"), None),
            P(),
            P(),
            P(),
        ),
        out_specs=(
            P("section", None, "tensor"),
            P("section", None, "tensor"),
            P(("section", "tensor"), None),
            P(),
        ),
        check_vma=False,
    )
```

profile of v0, /device:TPU:0, one launch (start us, length us, event | category | flops | bytes accessed | tf_op | source)
XLA Modules:
  0.0 578.9 jit_solution(3762362679505095675)
XLA Ops:
  8.1 12.4 %all-gather = bf16[1,128,2304]{1,2,0:T(8,128)(2,1)S(1)} all-gather(bf16[1,128,576]{1,2,0:T(8,128)(2,1)} %param.11), channel_id=2, replica_groups=mesh['section'=8,'tensor'=4] {'tensor'}, dimensions={2}, use_global_device_ids=true | all-gather | bytes 737280 | tf_op jit(solution)/shard_map/all_gather | solution.py:34
  30.5 21.3 %reduce-scatter.7.cloned.1.call-done = bf16[128,576]{0,1:T(8,128)(2,1)} async-done(((bf16[128,2304]{0,1:T(8,128)(2,1)}), bf16[128,576]{0,1:T(8,128)(2,1)}) %reduce-scatter.7.cloned.1.call-update) | async-done | bytes 147472 | tf_op jit(solution)/shard_map/reduce_scatter | solution.py:40
  53.5 2.3 collective-permute-start
  55.8 113.7 %all-reduce.14.cloned.1.call-done = (f32[128,2304]{0,1:T(8,128)}, f32[128,2304]{0,1:T(8,128)}) async-done(((f32[128,2304]{0,1:T(8,128)}, f32[128,2304]{0,1:T(8,128)}), (f32[128,2304]{0,1:T(8,128)}, f32[128,2304]{0,1:T(8,128)})) %all-reduce.14.cloned.1.call-update) | async-done | bytes 2359312 | tf_op jit(solution)/shard_map/psum | solution.py:64
  171.2 11.3 %all_gather.31 = bf16[128,2304]{0,1:T(8,128)(2,1)S(1)} all-gather(bf16[128,576]{0,1:T(8,128)(2,1)S(1)} %fusion.112), channel_id=1, replica_groups=mesh['section'=8,'tensor'=4] {'tensor'}, dimensions={1}, use_global_device_ids=true | all-gather | bytes 737280 | tf_op jit(solution)/shard_map/all_gather | solution.py:34
  185.9 2.2 convolution_convert_fusion.2
  188.2 10.5 %all_gather.33 = bf16[128,2304]{0,1:T(8,128)(2,1)S(1)} all-gather(bf16[128,576]{0,1:T(8,128)(2,1)} %add_convert_fusion.1), channel_id=1, replica_groups=mesh['section'=8,'tensor'=4] {'tensor'}, dimensions={1}, use_global_device_ids=true | all-gather | bytes 737280 | tf_op jit(solution)/shard_map/all_gather | solution.py:34
  199.5 13.0 %reduce-scatter.9.cloned.1.call-done = bf16[128,576]{0,1:T(8,128)(2,1)} async-done(((bf16[128,2304]{0,1:T(8,128)(2,1)}), bf16[128,576]{0,1:T(8,128)(2,1)}) %reduce-scatter.9.cloned.1.call-update) | async-done | bytes 147472 | tf_op jit(solution)/shard_map/reduce_scatter | solution.py:40
  214.2 10.2 %all_gather.32 = bf16[128,2304]{0,1:T(8,128)(2,1)S(1)} all-gather(bf16[128,576]{0,1:T(8,128)(2,1)S(1)} %add_convert_fusion), channel_id=1, replica_groups=mesh['section'=8,'tensor'=4] {'tensor'}, dimensions={1}, use_global_device_ids=true | all-gather | bytes 737280 | tf_op jit(solution)/shard_map/all_gather | solution.py:34
  228.3 11.7 %all-gather.2 = bf16[1,128,2304]{1,2,0:T(8,128)(2,1)} all-gather(bf16[1,128,576]{1,2,0:T(8,128)(2,1)} %param.12), channel_id=4, replica_groups=mesh['section'=8,'tensor'=4] {'tensor'}, dimensions={2}, use_global_device_ids=true | all-gather | bytes 737280 | tf_op jit(solution)/shard_map/all_gather | solution.py:34
  241.2 43.7 %all-reduce.20.cloned.1.call-done = (bf16[128,2304]{0,1:T(8,128)(2,1)}, bf16[128,2304]{0,1:T(8,128)(2,1)}) async-done(((bf16[128,2304]{0,1:T(8,128)(2,1)}, bf16[128,2304]{0,1:T(8,128)(2,1)}), (bf16[128,2304]{0,1:T(8,128)(2,1)}, bf16[128,2304]{0,1:T(8,128)(2,1)})) %all-reduce.20.cloned.1.call-update) | async-done | bytes 1179664 | tf_op jit(solution)/shard_map/psum | solution.py:28
  288.9 2.3 fusion.123
  291.1 10.7 %all-reduce.3 = (bf16[128]{0:T(256)(128)(2,1)}, bf16[128]{0:T(256)(128)(2,1)}) all-reduce(f32[128]{0:T(128)} %get-tuple-element.5, f32[128]{0:T(128)} %get-tuple-element.10), channel_id=1, replica_groups=mesh['section'=8,'tensor'=4] {'tensor'}, use_global_device_ids=true, to_apply=%region_20.21 | all-reduce | flops 256 | bytes 1536 | tf_op jit(solution)/shard_map/psum | solution.py:46
  301.8 14.3 %all-reduce.5 = (bf16[128]{0:T(256)(128)(2,1)}, bf16[128]{0:T(256)(128)(2,1)}) all-reduce(bf16[128]{0:T(256)(128)(2,1)} %get-tuple-element.21, bf16[128]{0:T(256)(128)(2,1)} %get-tuple-element.20), channel_id=1, replica_groups=mesh['section'=8,'tensor'=4] {'section'}, use_global_device_ids=true, to_apply=%region_12.13 | all-reduce | flops 256 | bytes 1024 | tf_op jit(solution)/shard_map/psum | solution.py:51
  317.4 2.4 convolution_convert_fusion.1
  319.8 12.8 %all-gather.1 = bf16[1,1,128,2304]{2,3,1,0:T(8,128)(2,1)S(1)} all-gather(bf16[1,1,128,576]{2,3,1,0:T(8,128)(2,1)} %slice.70), channel_id=3, replica_groups=mesh['section'=8,'tensor'=4] {'tensor'}, dimensions={3}, use_global_device_ids=true | all-gather | bytes 737280 | tf_op jit(solution)/shard_map/all_gather | solution.py:34
  342.8 10.7 %all_gather.36 = bf16[128,2304]{0,1:T(8,128)(2,1)S(1)} all-gather(bf16[128,576]{0,1:T(8,128)(2,1)S(1)} %bitcast_select_fusion), channel_id=1, replica_groups=mesh['section'=8,'tensor'=4] {'tensor'}, dimensions={1}, use_global_device_ids=true | all-gather | bytes 737280 | tf_op jit(solution)/shard_map/all_gather | solution.py:34
  356.7 13.5 %reduce-scatter.13.cloned.1.call-done = bf16[128,576]{0,1:T(8,128)(2,1)} async-done(((bf16[128,2304]{0,1:T(8,128)(2,1)}), bf16[128,576]{0,1:T(8,128)(2,1)}) %reduce-scatter.13.cloned.1.call-update) | async-done | bytes 147472 | tf_op jit(solution)/shard_map/reduce_scatter | solution.py:40
  375.4 22.8 %reduce-scatter.15.cloned.1.call-done = bf16[128,576]{0,1:T(8,128)(2,1)} async-done(((bf16[128,2304]{0,1:T(8,128)(2,1)}), bf16[128,576]{0,1:T(8,128)(2,1)}) %reduce-scatter.15.cloned.1.call-update) | async-done | bytes 147472 | tf_op jit(solution)/shard_map/reduce_scatter | solution.py:40
  402.2 21.0 %all-reduce.18.cloned.1.call-done = (bf16[128,576]{0,1:T(8,128)(2,1)}, bf16[128,576]{0,1:T(8,128)(2,1)}) async-done(((bf16[128,576]{0,1:T(8,128)(2,1)}, bf16[128,576]{0,1:T(8,128)(2,1)}), (bf16[128,576]{0,1:T(8,128)(2,1)}, bf16[128,576]{0,1:T(8,128)(2,1)})) %all-reduce.18.cloned.1.call-update) | async-done | bytes 294928 | tf_op jit(solution)/shard_map/psum | solution.py:51
  425.2 10.5 %all-reduce.2 = (f32[128]{0:T(128)}, f32[128]{0:T(128)}) all-reduce(f32[128]{0:T(128)} %fusion.101, f32[128]{0:T(128)} %get-tuple-element.9), channel_id=1, replica_groups=mesh['section'=8,'tensor'=4] {'tensor'}, use_global_device_ids=true, to_apply=%region_31.32 | all-reduce | flops 256 | bytes 2048 | tf_op jit(solution)/shard_map/psum | solution.py:46
  439.5 3.7 collective-permute-start.1
  444.5 11.0 %all_gather.37 = bf16[128,2304]{0,1:T(8,128)(2,1)S(1)} all-gather(bf16[128,576]{0,1:T(8,128)(2,1)S(1)} %fusion.113), channel_id=1, replica_groups=mesh['section'=8,'tensor'=4] {'tensor'}, dimensions={1}, use_global_device_ids=true | all-gather | bytes 737280 | tf_op jit(solution)/shard_map/all_gather | solution.py:34
  459.9 2.3 fusion.108
  462.3 13.0 %all_gather.38 = bf16[128,2304]{0,1:T(8,128)(2,1)S(1)} all-gather(bf16[128,576]{0,1:T(8,128)(2,1)S(1)} %copy-done.18), channel_id=1, replica_groups=mesh['section'=8,'tensor'=4] {'tensor'}, dimensions={1}, use_global_device_ids=true | all-gather | bytes 737280 | tf_op jit(solution)/shard_map/all_gather | solution.py:34
  476.2 7.2 %reduce-scatter.17.cloned.1.call-done = bf16[128,576]{0,1:T(8,128)(2,1)} async-done(((bf16[128,2304]{0,1:T(8,128)(2,1)}), bf16[128,576]{0,1:T(8,128)(2,1)}) %reduce-scatter.17.cloned.1.call-update) | async-done | bytes 147472 | tf_op jit(solution)/shard_map/reduce_scatter | solution.py:40
  484.6 9.3 %all-reduce.1 = (f32[128]{0:T(128)S(1)}, f32[128]{0:T(128)S(1)}, bf16[128]{0:T(256)(128)(2,1)S(1)}, bf16[128]{0:T(256)(128)(2,1)S(1)}) all-reduce(f32[128]{0:T(128)S(1)} %fusion.105, f32[128]{0:T(128)S(1)} %copy-done.55, f32[128]{0:T(128)S(1)} %copy-done.63, f32[128]{0:T(128)S(1)} %copy-done.62), channel_id=1, replica_groups=mesh['section'=8,'tensor'=4] {'tensor'}, use_global_device_ids=true, to_apply=%region_37.38 | all-reduce | flops 512 | bytes 3584 | tf_op jit(solution)/shard_map/psum | solution.py:46
  495.1 10.6 %all_gather.39 = bf16[128,2304]{0,1:T(8,128)(2,1)S(1)} all-gather(bf16[128,576]{0,1:T(8,128)(2,1)S(1)} %fusion.104), channel_id=1, replica_groups=mesh['section'=8,'tensor'=4] {'tensor'}, dimensions={1}, use_global_device_ids=true | all-gather | bytes 737280 | tf_op jit(solution)/shard_map/all_gather | solution.py:34
  506.7 2.3 fusion.109
  510.3 17.9 %all-reduce.4 = (bf16[128]{0:T(256)(128)(2,1)S(1)}, bf16[128]{0:T(256)(128)(2,1)S(1)}) all-reduce(bf16[128]{0:T(256)(128)(2,1)S(1)} %get-tuple-element.16, bf16[128]{0:T(256)(128)(2,1)S(1)} %get-tuple-element.17), channel_id=1, replica_groups=mesh['section'=8,'tensor'=4] {'section'}, use_global_device_ids=true, to_apply=%region_46.47 | all-reduce | flops 256 | bytes 1024 | tf_op jit(solution)/shard_map/psum | solution.py:51
  533.0 33.5 %all-reduce.16.cloned.1.call-done = (bf16[128,2304]{0,1:T(8,128)(2,1)}, bf16[128,2304]{0,1:T(8,128)(2,1)}) async-done(((bf16[128,2304]{0,1:T(8,128)(2,1)}, bf16[128,2304]{0,1:T(8,128)(2,1)}), (bf16[128,2304]{0,1:T(8,128)(2,1)}, bf16[128,2304]{0,1:T(8,128)(2,1)})) %all-reduce.16.cloned.1.call-update) | async-done | bytes 1179664 | tf_op jit(solution)/shard_map/psum | solution.py:28
  566.5 3.2 fusion.2
  (237 shorter events, 74.0 us)
Async XLA Ops:
  8.0 43.8 %reduce-scatter.7.cloned.1.call-start = ((), (), s32[]{:S(2)}) async-start(), calls=%async_computation.6 | async-start | bytes 737280 | tf_op jit(solution)/shard_map/reduce_scatter | solution.py:40
  26.3 143.2 %all-reduce.14.cloned.1.call-start = ((), (), s32[]{:S(2)}) async-start(), calls=%async_computation.12 | async-start | bytes 4718592 | tf_op jit(solution)/shard_map/psum | solution.py:64
  26.4 310.4 %copy-start.30 = (s32[256]{0:T(256)}, s32[256]{0:T(256)S(1)}, u32[]{:S(2)}) copy-start(s32[256]{0:T(256)S(1)} %iota_add_fusion) | copy-start | bytes 3076
  30.5 182.1 %reduce-scatter.9.cloned.1.call-start = ((), (), s32[]{:S(2)}) async-start(), calls=%async_computation.7 | async-start | bytes 737280 | tf_op jit(solution)/shard_map/reduce_scatter | solution.py:40
  53.5 116.0 %collective-permute-start = (bf16[128,576]{0,1:T(8,128)(2,1)}, bf16[128,576]{0,1:T(8,128)(2,1)}, u32[]{:S(2)}, u32[]{:S(2)}) collective-permute-start(bf16[128,576]{0,1:T(8,128)(2,1)} %add_convert_fusion.1), channel_id=1, source_target_pairs={{0,4},{4,8},{8,12},{12,16},{16,20},{20,24},{24,28},{1,5},{5,9},{9,... | collective-permute-start | bytes 442376 | tf_op jit(solution)/shard_map/ppermute | solution.py:23
  188.1 96.8 %all-reduce.20.cloned.1.call-start = ((), (), s32[]{:S(2)}) async-start(), calls=%async_computation.15 | async-start | bytes 2359296 | tf_op jit(solution)/shard_map/psum | solution.py:28
  225.3 131.3 %reduce-scatter.11.cloned.1.call-start = ((), (), s32[]{:S(2)}) async-start(), calls=%async_computation.8 | async-start | bytes 737280 | tf_op jit(solution)/shard_map/reduce_scatter | solution.py:40
  319.8 50.3 %reduce-scatter.13.cloned.1.call-start = ((), (), s32[]{:S(2)}) async-start(), calls=%async_computation.9 | async-start | bytes 737280 | tf_op jit(solution)/shard_map/reduce_scatter | solution.py:40
  338.7 59.5 %reduce-scatter.15.cloned.1.call-start = ((), (), s32[]{:S(2)}) async-start(), calls=%async_computation.10 | async-start | bytes 737280 | tf_op jit(solution)/shard_map/reduce_scatter | solution.py:40
  342.7 80.5 %all-reduce.18.cloned.1.call-start = ((), (), s32[]{:S(2)}) async-start(), calls=%async_computation.14 | async-start | bytes 589824 | tf_op jit(solution)/shard_map/psum | solution.py:51
  370.2 113.2 %reduce-scatter.17.cloned.1.call-start = ((), (), s32[]{:S(2)}) async-start(), calls=%async_computation.11 | async-start | bytes 737280 | tf_op jit(solution)/shard_map/reduce_scatter | solution.py:40
  373.3 26.6 %copy-start.8 = (bf16[128,2304]{0,1:T(8,128)(2,1)S(1)}, bf16[128,2304]{0,1:T(8,128)(2,1)}, u32[]{:S(2)}) copy-start(bf16[128,2304]{0,1:T(8,128)(2,1)} %get-tuple-element.30) | copy-start | bytes 1769476
  374.2 69.0 %copy-start.33 = (f32[576]{0:T(1024)}, f32[576]{0:T(1024)S(1)}, u32[]{:S(2)}) copy-start(f32[576]{0:T(1024)S(1)} %dynamic_slice.28) | copy-start | bytes 6916
  375.3 25.8 %copy-start.6 = (bf16[128,2304]{0,1:T(8,128)(2,1)S(1)}, bf16[128,2304]{0,1:T(8,128)(2,1)}, u32[]{:S(2)}) copy-start(bf16[128,2304]{0,1:T(8,128)(2,1)} %get-tuple-element.31) | copy-start | bytes 1769476
  401.1 34.5 %copy-start.59 = (f32[128]{0:T(128)S(1)}, f32[128]{0:T(128)}, u32[]{:S(2)}) copy-start(f32[128]{0:T(128)} %copy-done.58) | copy-start | bytes 1540
  402.2 41.0 %copy-start.47 = (f32[128]{0:T(128)S(1)}, f32[128]{0:T(128)}, u32[]{:S(2)}) copy-start(f32[128]{0:T(128)} %copy-done.46) | copy-start | bytes 1540
  436.9 6.3 %collective-permute-start.2 = (bf16[128,576]{0,1:T(8,128)(2,1)S(1)}, bf16[128,576]{0,1:T(8,128)(2,1)S(1)}, u32[]{:S(2)}, u32[]{:S(2)}) collective-permute-start(bf16[128,576]{0,1:T(8,128)(2,1)S(1)} %fusion.100), channel_id=1, source_target_pairs={{4,0},{8,4},{12,8},{16,12},{20,16},{24,20},{28,24},{5,1},{9,5},{13... | collective-permute-start | bytes 442376 | tf_op jit(solution)/shard_map/ppermute | solution.py:23
  439.5 18.7 %collective-permute-start.1 = (bf16[128,576]{0,1:T(8,128)(2,1)}, bf16[128,576]{0,1:T(8,128)(2,1)}, u32[]{:S(2)}, u32[]{:S(2)}) collective-permute-start(bf16[128,576]{0,1:T(8,128)(2,1)} %copy-done.15), channel_id=1, source_target_pairs={{0,4},{4,8},{8,12},{12,16},{16,20},{20,24},{24,28},{1,5},{5,9},{9,... | collective-permute-start | bytes 442376 | tf_op jit(solution)/shard_map/ppermute | solution.py:23
  458.1 108.4 %all-reduce.16.cloned.1.call-start = ((), (), s32[]{:S(2)}) async-start(), calls=%async_computation.13 | async-start | bytes 2359296 | tf_op jit(solution)/shard_map/psum | solution.py:28
  462.2 22.3 %copy-start.55 = (f32[128]{0:T(128)S(1)}, f32[128]{0:T(128)}, u32[]{:S(2)}) copy-start(f32[128]{0:T(128)} %get-tuple-element.8) | copy-start | bytes 1540
  462.2 22.3 %copy-start.62 = (f32[128]{0:T(128)S(1)}, f32[128]{0:T(128)}, u32[]{:S(2)}) copy-start(f32[128]{0:T(128)} %get-tuple-element.4) | copy-start | bytes 1540
  462.2 22.3 %copy-start.63 = (f32[128]{0:T(128)S(1)}, f32[128]{0:T(128)}, u32[]{:S(2)}) copy-start(f32[128]{0:T(128)} %get-tuple-element.11) | copy-start | bytes 1540
  462.2 31.6 %copy-start.12 = (bf16[128,576]{0,1:T(8,128)(2,1)S(1)}, bf16[128,576]{0,1:T(8,128)(2,1)}, u32[]{:S(2)}) copy-start(bf16[128,576]{0,1:T(8,128)(2,1)} %copy-done.11) | copy-start | bytes 442372
  462.2 31.6 %copy-start.57 = (f32[128]{0:T(128)S(1)}, f32[128]{0:T(128)}, u32[]{:S(2)}) copy-start(f32[128]{0:T(128)} %copy-done.56) | copy-start | bytes 1540
  462.3 31.6 %copy-start.64 = (f32[128]{0:T(128)S(1)}, f32[128]{0:T(128)}, u32[]{:S(2)}) copy-start(f32[128]{0:T(128)} %get-tuple-element.40) | copy-start | bytes 1540
  506.7 22.1 %copy-start.66 = (bf16[128]{0:T(256)(128)(2,1)S(1)}, bf16[128]{0:T(256)(128)(2,1)}, u32[]{:S(2)}) copy-start(bf16[128]{0:T(256)(128)(2,1)} %get-tuple-element.25) | copy-start | bytes 772
  506.7 24.5 %copy-start.16 = (bf16[128,576]{0,1:T(8,128)(2,1)S(1)}, bf16[128,576]{0,1:T(8,128)(2,1)}, u32[]{:S(2)}) copy-start(bf16[128,576]{0,1:T(8,128)(2,1)} %get-tuple-element.28) | copy-start | bytes 442372
  506.7 24.5 %copy-start.34 = (f32[576]{0:T(1024)S(1)}, f32[576]{0:T(1024)}, u32[]{:S(2)}) copy-start(f32[576]{0:T(1024)} %copy-done.33) | copy-start | bytes 6916
  506.7 24.5 %copy-start.45 = (f32[128]{0:T(128)S(1)}, f32[128]{0:T(128)}, u32[]{:S(2)}) copy-start(f32[128]{0:T(128)} %copy-done.43) | copy-start | bytes 1540
  506.7 24.5 %copy-start.60 = (f32[128]{0:T(128)S(1)}, f32[128]{0:T(128)}, u32[]{:S(2)}) copy-start(f32[128]{0:T(128)} %get-tuple-element.38) | copy-start | bytes 1540
  506.7 59.8 %copy-start.54 = (s32[128]{0:T(128)S(1)}, s32[128]{0:T(128)}, u32[]{:S(2)}) copy-start(s32[128]{0:T(128)} %get-tuple-element.33) | copy-start | bytes 1540
  509.0 22.2 %collective-permute-start.3 = (bf16[128,576]{0,1:T(8,128)(2,1)S(1)}, bf16[128,576]{0,1:T(8,128)(2,1)S(1)}, u32[]{:S(2)}, u32[]{:S(2)}) collective-permute-start(bf16[128,576]{0,1:T(8,128)(2,1)S(1)} %fusion.104), channel_id=1, source_target_pairs={{4,0},{8,4},{12,8},{16,12},{20,16},{24,20},{28,24},{5,1},{9,5},{13... | collective-permute-start | bytes 442376 | tf_op jit(solution)/shard_map/ppermute | solution.py:23
  (50 other events, 195.4 us)
Sparse Core Ops, SparseCore 0:
  26.4 25.3 reduce-scatter.6
  188.2 24.2 reduce-scatter.8
  319.9 22.2 reduce-scatter.10
  344.9 25.1 reduce-scatter.12
  373.1 25.1 reduce-scatter.14
  458.2 25.0 reduce-scatter.16
Sparse Core Ops, SparseCore 1:
  34.0 135.5 all-reduce.13
  225.4 59.5 all-reduce.19
  370.2 52.9 all-reduce.17
  506.7 59.8 all-reduce.15
where the time goes:
time: 580 us; the launch traced here: 579 us
  waiting for transfers between devices  290 us (50%)
  blocking collectives  177 us (31%)
  matrix products  41.2 us (7%)
  other arithmetic  33.3 us (6%)
  between operations  17.7 us (3%)
  local copies, waits for them, and re-layouts  10.9 us (2%)
  starting transfers between devices  8.97 us (2%)
    all_gather x10, blocking collectives, widen(): lax.all_gather(for_sending(values), 'tensor', axis=1, tiled=True)  114 us
    psum x1, waiting for transfers between devices, reduce_lookup(): summed = lax.psum(parts, ('section', 'tensor'))  114 us
    reduce_scatter x6, waiting for transfers between devices, sum_width(): lax.psum_scatter(term.astype(jnp.bfloat16), 'tensor', scatter_dimension=1...  77.8 us
    psum x2, waiting for transfers between devices, broadcast(): return lax.psum(block, axis)  77.3 us
    psum x2, blocking collectives, sum_section(): lax.psum(for_sending(values), 'section')  32.2 us
    psum x3, blocking collectives, stat_width(): return lax.psum(values, 'tensor')  30.4 us
    psum x1, waiting for transfers between devices, sum_section(): lax.psum(for_sending(values), 'section')  21 us
  transfers between devices with their start and end apart: 14, of which 9 were waited for; matrix products, arithmetic and copies ran while one was open for 8% of the time, Pallas kernels for 0%

commit v1 on v0

--- a/solution.py
+++ b/solution.py
@@ -9,6 +9,12 @@
 LOGIT_CAP = 30.0
 
 
+def summed_here(block, axis):
+    shards = lax.all_gather(block, axis, axis=0, tiled=False)
+    summed = shards.sum(axis=0)
+    return summed
+
+
 def for_sending(x):
 
     def short(part):
@@ -25,7 +31,7 @@
 
 def broadcast(block, axis, holder):
     block = jnp.where(lax.axis_index(axis) == holder, block, jnp.zeros_like(block))
-    return lax.psum(block, axis)
+    return summed_here(block, axis)
 
 
 def widen(values):

time: 580 us -> 695 us (1.20)
  waiting for transfers between devices: 290 us -> 344 us
  other arithmetic: 33.3 us -> 72.2 us
  local copies, waits for them, and re-layouts: 10.9 us -> 24.1 us
  blocking collectives: 177 us -> 186 us
    all_gather x0 -> x4, waiting for transfers between devices: none -> 85.6 us  [summed_here(): shards = lax.all_gather(block, axis, axis=0, tiled=False)]
    psum x2 -> x0, waiting for transfers between devices: 77.3 us -> none  [broadcast(): return lax.psum(block, axis)]
    reduce_sum x0 -> x4, other arithmetic: none -> 39.4 us  [summed_here(): summed = shards.sum(axis=0)]
    psum x1, waiting for transfers between devices: 21 us -> 51.5 us  [sum_section(): lax.psum(for_sending(values), 'section')]
    unnamed x136 -> x134, local copies, waits for them, and re-layouts: 5 us -> 19.6 us
    reduce_scatter x6, waiting for transfers between devices: 77.8 us -> 91.9 us  [sum_width(): lax.psum_scatter(term.astype(jnp.bfloat16), 'tensor', scatter_dimension=1...]
    psum x2, blocking collectives: 32.2 us -> 45.2 us  [sum_section(): lax.psum(for_sending(values), 'section')]
  transfers between devices with their start and end apart: 14 -> 16, of which waited for: 9 -> 11; matrix products, arithmetic and copies ran while one was open for 8% -> 11% of each run, Pallas kernels for 0% -> 0%
where the time goes in v1:
time: 695 us; the launch traced here: 689 us
  waiting for transfers between devices  344 us (49%)
  blocking collectives  186 us (27%)
  other arithmetic  72.2 us (10%)
  matrix products  39 us (6%)
  local copies, waits for them, and re-layouts  24.1 us (3%)
  between operations  17.7 us (3%)
    psum x1, waiting for transfers between devices, reduce_lookup(): summed = lax.psum(parts, ('section', 'tensor'))  114 us
    all_gather x10, blocking collectives, widen(): lax.all_gather(for_sending(values), 'tensor', axis=1, tiled=True)  110 us
    reduce_scatter x6, waiting for transfers between devices, sum_width(): lax.psum_scatter(term.astype(jnp.bfloat16), 'tensor', scatter_dimension=1...  91.9 us
    all_gather x4, waiting for transfers between devices, summed_here(): shards = lax.all_gather(block, axis, axis=0, tiled=False)  85.6 us
    psum x1, waiting for transfers between devices, sum_section(): lax.psum(for_sending(values), 'section')  51.5 us
    psum x2, blocking collectives, sum_section(): lax.psum(for_sending(values), 'section')  45.2 us
    reduce_sum x4, other arithmetic, summed_here(): summed = shards.sum(axis=0)  39.4 us
    psum x3, blocking collectives, stat_width(): return lax.psum(values, 'tensor')  30.9 us
  transfers between devices with their start and end apart: 16, of which 11 were waited for; matrix products, arithmetic and copies ran while one was open for 11% of the time, Pallas kernels for 0%

profile of v1, /device:TPU:0, one launch (start us, length us, event | category | flops | bytes accessed | tf_op | source)
XLA Modules:
  0.0 689.4 jit_solution(9370363107602811037)
XLA Ops:
  8.9 12.3 %all-gather = bf16[1,128,2304]{1,2,0:T(8,128)(2,1)S(1)} all-gather(bf16[1,128,576]{1,2,0:T(8,128)(2,1)} %param.11), channel_id=2, replica_groups=mesh['section'=8,'tensor'=4] {'tensor'}, dimensions={2}, use_global_device_ids=true | all-gather | bytes 737280 | tf_op jit(solution)/shard_map/all_gather | solution.py:40
  30.5 21.3 %reduce-scatter.7.cloned.1.call-done = bf16[128,576]{0,1:T(8,128)(2,1)} async-done(((bf16[128,2304]{0,1:T(8,128)(2,1)}), bf16[128,576]{0,1:T(8,128)(2,1)}) %reduce-scatter.7.cloned.1.call-update) | async-done | bytes 147472 | tf_op jit(solution)/shard_map/reduce_scatter | solution.py:46
  55.7 113.8 %all-reduce.10.cloned.1.call-done = (f32[128,2304]{0,1:T(8,128)}, f32[128,2304]{0,1:T(8,128)}) async-done(((f32[128,2304]{0,1:T(8,128)}, f32[128,2304]{0,1:T(8,128)}), (f32[128,2304]{0,1:T(8,128)}, f32[128,2304]{0,1:T(8,128)})) %all-reduce.10.cloned.1.call-update) | async-done | bytes 2359312 | tf_op jit(solution)/shard_map/psum | solution.py:70
  171.2 11.3 %all_gather.55 = bf16[128,2304]{0,1:T(8,128)(2,1)S(1)} all-gather(bf16[128,576]{0,1:T(8,128)(2,1)S(1)} %fusion.112), channel_id=1, replica_groups=mesh['section'=8,'tensor'=4] {'tensor'}, dimensions={1}, use_global_device_ids=true | all-gather | bytes 737280 | tf_op jit(solution)/shard_map/all_gather | solution.py:40
  188.2 10.5 %all_gather.59 = bf16[128,2304]{0,1:T(8,128)(2,1)S(1)} all-gather(bf16[128,576]{0,1:T(8,128)(2,1)} %add_convert_fusion.1), channel_id=1, replica_groups=mesh['section'=8,'tensor'=4] {'tensor'}, dimensions={1}, use_global_device_ids=true | all-gather | bytes 737280 | tf_op jit(solution)/shard_map/all_gather | solution.py:40
  199.6 12.9 %reduce-scatter.9.cloned.1.call-done = bf16[128,576]{0,1:T(8,128)(2,1)} async-done(((bf16[128,2304]{0,1:T(8,128)(2,1)}), bf16[128,576]{0,1:T(8,128)(2,1)}) %reduce-scatter.9.cloned.1.call-update) | async-done | bytes 147472 | tf_op jit(solution)/shard_map/reduce_scatter | solution.py:46
  214.2 10.2 %all_gather.56 = bf16[128,2304]{0,1:T(8,128)(2,1)S(1)} all-gather(bf16[128,576]{0,1:T(8,128)(2,1)S(1)} %add_convert_fusion), channel_id=1, replica_groups=mesh['section'=8,'tensor'=4] {'tensor'}, dimensions={1}, use_global_device_ids=true | all-gather | bytes 737280 | tf_op jit(solution)/shard_map/all_gather | solution.py:40
  227.5 11.1 %all-gather.3 = bf16[1,1,128,2304]{2,3,1,0:T(8,128)(2,1)} all-gather(bf16[1,1,128,576]{2,3,1,0:T(8,128)(2,1)S(1)} %slice.70), channel_id=5, replica_groups=mesh['section'=8,'tensor'=4] {'tensor'}, dimensions={3}, use_global_device_ids=true | all-gather | bytes 737280 | tf_op jit(solution)/shard_map/all_gather | solution.py:40
  240.0 26.4 %all-gather.14.cloned.1.call-done = bf16[1024,2304]{0,1:T(8,128)(2,1)} async-done(((bf16[128,2304]{0,1:T(8,128)(2,1)}), bf16[1024,2304]{0,1:T(8,128)(2,1)}) %all-gather.14.cloned.1.call-update) | async-done | bytes 4718608 | tf_op jit(solution)/shard_map/all_gather | solution.py:13
  266.3 3.6 copy.32
  269.9 9.8 %bitcast_reduce_fusion.2 = bf16[128,2304]{0,1:T(8,128)(2,1)S(1)} fusion(bf16[288,8,8,128]{3,2,1,0:T(8,128)(2,1)S(1)} %copy.32), kind=kLoop, calls=%fused_computation.2 | loop fusion | flops 2064384 | bytes 5308416 | tf_op jit(solution)/shard_map/reduce_sum | solution.py:14
  281.4 37.4 %all-gather.12.cloned.1.call-done = bf16[1024,2304]{0,1:T(8,128)(2,1)} async-done(((bf16[128,2304]{0,1:T(8,128)(2,1)}), bf16[1024,2304]{0,1:T(8,128)(2,1)}) %all-gather.12.cloned.1.call-update) | async-done | bytes 4718608 | tf_op jit(solution)/shard_map/all_gather | solution.py:13
  318.9 3.6 copy.31
  322.4 9.8 %bitcast_reduce_fusion.3 = bf16[128,2304]{0,1:T(8,128)(2,1)S(1)} fusion(bf16[288,8,8,128]{3,2,1,0:T(8,128)(2,1)S(1)} %copy.31), kind=kLoop, calls=%fused_computation.3 | loop fusion | flops 2064384 | bytes 5308416 | tf_op jit(solution)/shard_map/reduce_sum | solution.py:14
  336.6 10.6 %all-reduce.3 = (bf16[128]{0:T(256)(128)(2,1)}, bf16[128]{0:T(256)(128)(2,1)}) all-reduce(f32[128]{0:T(128)} %get-tuple-element.5, f32[128]{0:T(128)} %get-tuple-element.10), channel_id=1, replica_groups=mesh['section'=8,'tensor'=4] {'tensor'}, use_global_device_ids=true, to_apply=%region_20.21 | all-reduce | flops 256 | bytes 1536 | tf_op jit(solution)/shard_map/psum | solution.py:52
  347.2 14.3 %all-reduce.5 = (bf16[128]{0:T(256)(128)(2,1)}, bf16[128]{0:T(256)(128)(2,1)}) all-reduce(bf16[128]{0:T(256)(128)(2,1)} %get-tuple-element.21, bf16[128]{0:T(256)(128)(2,1)} %get-tuple-element.20), channel_id=1, replica_groups=mesh['section'=8,'tensor'=4] {'section'}, use_global_device_ids=true, to_apply=%region_12.13 | all-reduce | flops 256 | bytes 1024 | tf_op jit(solution)/shard_map/psum | solution.py:57
  365.1 13.4 %all-gather.4 = bf16[1,128,2304]{1,2,0:T(8,128)(2,1)S(1)} all-gather(bf16[1,128,576]{1,2,0:T(8,128)(2,1)} %param.12), channel_id=6, replica_groups=mesh['section'=8,'tensor'=4] {'tensor'}, dimensions={2}, use_global_device_ids=true | all-gather | bytes 737280 | tf_op jit(solution)/shard_map/all_gather | solution.py:40
  389.2 9.1 %all_gather.64 = bf16[128,2304]{0,1:T(8,128)(2,1)S(1)} all-gather(bf16[128,576]{0,1:T(8,128)(2,1)S(1)} %bitcast_select_fusion), channel_id=1, replica_groups=mesh['section'=8,'tensor'=4] {'tensor'}, dimensions={1}, use_global_device_ids=true | all-gather | bytes 737280 | tf_op jit(solution)/shard_map/all_gather | solution.py:40
  399.2 17.4 %reduce-scatter.11.cloned.1.call-done = bf16[128,576]{0,1:T(8,128)(2,1)} async-done(((bf16[128,2304]{0,1:T(8,128)(2,1)}), bf16[128,576]{0,1:T(8,128)(2,1)}) %reduce-scatter.11.cloned.1.call-update) | async-done | bytes 147472 | tf_op jit(solution)/shard_map/reduce_scatter | solution.py:46
  419.7 25.1 %reduce-scatter.15.cloned.1.call-done = bf16[128,576]{0,1:T(8,128)(2,1)} async-done(((bf16[128,2304]{0,1:T(8,128)(2,1)}), bf16[128,576]{0,1:T(8,128)(2,1)}) %reduce-scatter.15.cloned.1.call-update) | async-done | bytes 147472 | tf_op jit(solution)/shard_map/reduce_scatter | solution.py:46
  448.7 51.5 %all-reduce.12.cloned.1.call-done = (bf16[128,576]{0,1:T(8,128)(2,1)}, bf16[128,576]{0,1:T(8,128)(2,1)}) async-done(((bf16[128,576]{0,1:T(8,128)(2,1)}, bf16[128,576]{0,1:T(8,128)(2,1)}), (bf16[128,576]{0,1:T(8,128)(2,1)}, bf16[128,576]{0,1:T(8,128)(2,1)})) %all-reduce.12.cloned.1.call-update) | async-done | bytes 294928 | tf_op jit(solution)/shard_map/psum | solution.py:57
  502.2 10.5 %all-reduce.2 = (f32[128]{0:T(128)}, f32[128]{0:T(128)}) all-reduce(f32[128]{0:T(128)} %fusion.101, f32[128]{0:T(128)} %get-tuple-element.9), channel_id=1, replica_groups=mesh['section'=8,'tensor'=4] {'tensor'}, use_global_device_ids=true, to_apply=%region_31.32 | all-reduce | flops 256 | bytes 2048 | tf_op jit(solution)/shard_map/psum | solution.py:52
  518.4 10.3 %all_gather.65 = bf16[128,2304]{0,1:T(8,128)(2,1)S(1)} all-gather(bf16[128,576]{0,1:T(8,128)(2,1)S(1)} %fusion.113), channel_id=1, replica_groups=mesh['section'=8,'tensor'=4] {'tensor'}, dimensions={1}, use_global_device_ids=true | all-gather | bytes 737280 | tf_op jit(solution)/shard_map/all_gather | solution.py:40
  531.3 10.5 %all_gather.66 = bf16[128,2304]{0,1:T(8,128)(2,1)S(1)} all-gather(bf16[128,576]{0,1:T(8,128)(2,1)} %copy-done.22), channel_id=1, replica_groups=mesh['section'=8,'tensor'=4] {'tensor'}, dimensions={1}, use_global_device_ids=true | all-gather | bytes 737280 | tf_op jit(solution)/shard_map/all_gather | solution.py:40
  544.0 15.3 %reduce-scatter.17.cloned.1.call-done = bf16[128,576]{0,1:T(8,128)(2,1)} async-done(((bf16[128,2304]{0,1:T(8,128)(2,1)}), bf16[128,576]{0,1:T(8,128)(2,1)}) %reduce-scatter.17.cloned.1.call-update) | async-done | bytes 147472 | tf_op jit(solution)/shard_map/reduce_scatter | solution.py:46
  560.4 9.8 %all-reduce.1 = (f32[128]{0:T(128)S(1)}, f32[128]{0:T(128)}, bf16[128]{0:T(256)(128)(2,1)}, bf16[128]{0:T(256)(128)(2,1)}) all-reduce(f32[128]{0:T(128)S(1)} %fusion.105, f32[128]{0:T(128)S(1)} %copy-done.53, f32[128]{0:T(128)} %get-tuple-element.11, f32[128]{0:T(128)} %get-tuple-element.4), channel_id=1, replica_groups=mesh['section'=8,'tensor'=4] {'tensor'}, use_global_device_ids=true, to_apply=%region_37.38 | all-reduce | flops 512 | bytes 3584 | tf_op jit(solution)/shard_map/psum | solution.py:52
  572.2 10.9 %all_gather.69 = bf16[128,2304]{0,1:T(8,128)(2,1)S(1)} all-gather(bf16[128,576]{0,1:T(8,128)(2,1)S(1)} %fusion.104), channel_id=1, replica_groups=mesh['section'=8,'tensor'=4] {'tensor'}, dimensions={1}, use_global_device_ids=true | all-gather | bytes 737280 | tf_op jit(solution)/shard_map/all_gather | solution.py:40
  594.5 30.9 %all-reduce.4 = (bf16[128]{0:T(256)(128)(2,1)S(1)}, bf16[128]{0:T(256)(128)(2,1)S(1)}) all-reduce(bf16[128]{0:T(256)(128)(2,1)S(1)} %copy-done.63, bf16[128]{0:T(256)(128)(2,1)S(1)} %copy-done.64), channel_id=1, replica_groups=mesh['section'=8,'tensor'=4] {'section'}, use_global_device_ids=true, to_apply=%region_46.47 | all-reduce | flops 256 | bytes 1024 | tf_op jit(solution)/shard_map/psum | solution.py:57
  629.7 3.6 copy.33
  633.3 9.8 %bitcast_reduce_fusion.1 = bf16[128,2304]{0,1:T(8,128)(2,1)S(1)} fusion(bf16[288,8,8,128]{3,2,1,0:T(8,128)(2,1)S(1)} %copy.33), kind=kLoop, calls=%fused_computation.1 | loop fusion | flops 2064384 | bytes 5308416 | tf_op jit(solution)/shard_map/reduce_sum | solution.py:14
  645.2 21.9 %all-gather.18.cloned.1.call-done = bf16[1024,2304]{0,1:T(8,128)(2,1)} async-done(((bf16[128,2304]{0,1:T(8,128)(2,1)}), bf16[1024,2304]{0,1:T(8,128)(2,1)}) %all-gather.18.cloned.1.call-update) | async-done | bytes 4718608 | tf_op jit(solution)/shard_map/all_gather | solution.py:13
  670.6 9.8 %bitcast_reduce_fusion = bf16[128,2304]{0,1:T(8,128)(2,1)S(1)} fusion(bf16[288,8,8,128]{3,2,1,0:T(8,128)(2,1)S(1)} %copy.34), kind=kLoop, calls=%fused_computation | loop fusion | flops 2064384 | bytes 5308416 | tf_op jit(solution)/shard_map/reduce_sum | solution.py:14
  (245 shorter events, 93.3 us)
Async XLA Ops:
  8.0 13.5 %copy-start = (bf16[1,2304,3,1,128]{4,1,3,2,0:T(8,128)(2,1)S(1)}, bf16[1,2304,3,1,128]{4,1,3,2,0:T(8,128)(2,1)}, u32[]{:S(2)}) copy-start(bf16[1,2304,3,1,128]{4,1,3,2,0:T(8,128)(2,1)} %param.14) | copy-start | bytes 5308420
  8.0 43.8 %reduce-scatter.7.cloned.1.call-start = ((), (), s32[]{:S(2)}) async-start(), calls=%async_computation.6 | async-start | bytes 737280 | tf_op jit(solution)/shard_map/reduce_scatter | solution.py:46
  26.3 143.2 %all-reduce.10.cloned.1.call-start = ((), (), s32[]{:S(2)}) async-start(), calls=%async_computation.16 | async-start | bytes 4718592 | tf_op jit(solution)/shard_map/psum | solution.py:70
  30.5 182.0 %reduce-scatter.9.cloned.1.call-start = ((), (), s32[]{:S(2)}) async-start(), calls=%async_computation.7 | async-start | bytes 737280 | tf_op jit(solution)/shard_map/reduce_scatter | solution.py:46
  53.5 116.0 %collective-permute-start = (bf16[128,576]{0,1:T(8,128)(2,1)}, bf16[128,576]{0,1:T(8,128)(2,1)}, u32[]{:S(2)}, u32[]{:S(2)}) collective-permute-start(bf16[128,576]{0,1:T(8,128)(2,1)} %add_convert_fusion.1), channel_id=1, source_target_pairs={{0,4},{4,8},{8,12},{12,16},{16,20},{20,24},{24,28},{1,5},{5,9},{9,... | collective-permute-start | bytes 442376 | tf_op jit(solution)/shard_map/ppermute | solution.py:29
  188.1 78.3 %all-gather.14.cloned.1.call-start = ((), (), s32[]{:S(2)}) async-start(), calls=%async_computation.13 | async-start | bytes 5308416 | tf_op jit(solution)/shard_map/all_gather | solution.py:13
  199.5 119.3 %all-gather.12.cloned.1.call-start = ((), (), s32[]{:S(2)}) async-start(), calls=%async_computation.12 | async-start | bytes 5308416 | tf_op jit(solution)/shard_map/all_gather | solution.py:13
  225.3 173.9 %reduce-scatter.13.cloned.1.call-start = ((), (), s32[]{:S(2)}) async-start(), calls=%async_computation.9 | async-start | bytes 737280 | tf_op jit(solution)/shard_map/reduce_scatter | solution.py:46
  365.0 51.5 %reduce-scatter.11.cloned.1.call-start = ((), (), s32[]{:S(2)}) async-start(), calls=%async_computation.8 | async-start | bytes 737280 | tf_op jit(solution)/shard_map/reduce_scatter | solution.py:46
  365.1 15.3 %copy-start.8 = (bf16[1,1,128,2304]{2,3,1,0:T(8,128)(2,1)S(1)}, bf16[1,1,128,2304]{2,3,1,0:T(8,128)(2,1)}, u32[]{:S(2)}) copy-start(bf16[1,1,128,2304]{2,3,1,0:T(8,128)(2,1)} %all-gather.3) | copy-start | bytes 1769476
  385.1 59.7 %reduce-scatter.15.cloned.1.call-start = ((), (), s32[]{:S(2)}) async-start(), calls=%async_computation.10 | async-start | bytes 737280 | tf_op jit(solution)/shard_map/reduce_scatter | solution.py:46
  389.1 111.1 %all-reduce.12.cloned.1.call-start = ((), (), s32[]{:S(2)}) async-start(), calls=%async_computation.17 | async-start | bytes 589824 | tf_op jit(solution)/shard_map/psum | solution.py:57
  398.3 18.3 %copy-start.10 = (bf16[128,2304]{0,1:T(8,128)(2,1)}, bf16[128,2304]{0,1:T(8,128)(2,1)S(1)}, u32[]{:S(2)}) copy-start(bf16[128,2304]{0,1:T(8,128)(2,1)S(1)} %all_gather.64) | copy-start | bytes 1769476
  399.2 19.2 %copy-start.56 = (f32[128]{0:T(128)}, f32[128]{0:T(128)S(1)}, u32[]{:S(2)}) copy-start(f32[128]{0:T(128)S(1)} %get-tuple-element.37) | copy-start | bytes 1540
  416.6 142.6 %reduce-scatter.17.cloned.1.call-start = ((), (), s32[]{:S(2)}) async-start(), calls=%async_computation.11 | async-start | bytes 737280 | tf_op jit(solution)/shard_map/reduce_scatter | solution.py:46
  418.4 28.1 %copy-start.5 = (bf16[128,2304]{0,1:T(8,128)(2,1)S(1)}, bf16[128,2304]{0,1:T(8,128)(2,1)}, u32[]{:S(2)}) copy-start(bf16[128,2304]{0,1:T(8,128)(2,1)} %copy-done.3) | copy-start | bytes 1769476
  418.5 98.7 %copy-start.34 = (f32[576]{0:T(1024)}, f32[576]{0:T(1024)S(1)}, u32[]{:S(2)}) copy-start(f32[576]{0:T(1024)S(1)} %dynamic_slice.28) | copy-start | bytes 6916
  419.6 28.0 %copy-start.7 = (bf16[128,2304]{0,1:T(8,128)(2,1)S(1)}, bf16[128,2304]{0,1:T(8,128)(2,1)}, u32[]{:S(2)}) copy-start(bf16[128,2304]{0,1:T(8,128)(2,1)} %copy-done.6) | copy-start | bytes 1769476
  448.7 68.5 %copy-start.47 = (f32[128]{0:T(128)S(1)}, f32[128]{0:T(128)}, u32[]{:S(2)}) copy-start(f32[128]{0:T(128)} %get-tuple-element.39) | copy-start | bytes 1540
  513.9 3.3 collective-permute-start.2
  531.3 11.6 %copy-start.11 = (bf16[128,2304]{0,1:T(8,128)(2,1)S(1)}, bf16[128,2304]{0,1:T(8,128)(2,1)}, u32[]{:S(2)}) copy-start(bf16[128,2304]{0,1:T(8,128)(2,1)} %copy-done.10) | copy-start | bytes 1769476
  531.3 98.4 %all-gather.16.cloned.1.call-start = ((), (), s32[]{:S(2)}) async-start(), calls=%async_computation.14 | async-start | bytes 5308416 | tf_op jit(solution)/shard_map/all_gather | solution.py:13
  542.8 17.6 %copy-start.53 = (f32[128]{0:T(128)S(1)}, f32[128]{0:T(128)}, u32[]{:S(2)}) copy-start(f32[128]{0:T(128)} %get-tuple-element.8) | copy-start | bytes 1540
  542.8 124.3 %all-gather.18.cloned.1.call-start = ((), (), s32[]{:S(2)}) async-start(), calls=%async_computation.15 | async-start | bytes 5308416 | tf_op jit(solution)/shard_map/all_gather | solution.py:13
  584.0 2.7 collective-permute-start.1
  590.8 34.6 %copy-start.61 = (bf16[128]{0:T(256)(128)(2,1)S(1)}, bf16[128]{0:T(256)(128)(2,1)}, u32[]{:S(2)}) copy-start(bf16[128]{0:T(256)(128)(2,1)} %get-tuple-element.24) | copy-start | bytes 772
  590.8 34.6 %copy-start.62 = (bf16[128]{0:T(256)(128)(2,1)S(1)}, bf16[128]{0:T(256)(128)(2,1)}, u32[]{:S(2)}) copy-start(bf16[128]{0:T(256)(128)(2,1)} %get-tuple-element.25) | copy-start | bytes 772
  590.8 37.1 %copy-start.19 = (bf16[128,576]{0,1:T(8,128)(2,1)S(1)}, bf16[128,576]{0,1:T(8,128)(2,1)}, u32[]{:S(2)}) copy-start(bf16[128,576]{0,1:T(8,128)(2,1)} %get-tuple-element.26) | copy-start | bytes 442372
  590.8 37.1 %copy-start.35 = (f32[576]{0:T(1024)S(1)}, f32[576]{0:T(1024)}, u32[]{:S(2)}) copy-start(f32[576]{0:T(1024)} %copy-done.34) | copy-start | bytes 6916
  590.8 37.1 %copy-start.58 = (f32[128]{0:T(128)S(1)}, f32[128]{0:T(128)}, u32[]{:S(2)}) copy-start(f32[128]{0:T(128)} %get-tuple-element.34) | copy-start | bytes 1540
  590.8 37.1 %copy-start.59 = (f32[128]{0:T(128)S(1)}, f32[128]{0:T(128)}, u32[]{:S(2)}) copy-start(f32[128]{0:T(128)} %get-tuple-element.15) | copy-start | bytes 1540
  593.2 34.7 %collective-permute-start.3 = (bf16[128,576]{0,1:T(8,128)(2,1)S(1)}, bf16[128,576]{0,1:T(8,128)(2,1)S(1)}, u32[]{:S(2)}, u32[]{:S(2)}) collective-permute-start(bf16[128,576]{0,1:T(8,128)(2,1)S(1)} %copy-done.21), channel_id=1, source_target_pairs={{4,0},{8,4},{12,8},{16,12},{20,16},{24,20},{28,24},{5,1},{9,5},{13... | collective-permute-start | bytes 442376 | tf_op jit(solution)/shard_map/ppermute | solution.py:29
  (49 other events, 169.7 us)
Sparse Core Ops, SparseCore 0:
  26.4 25.3 reduce-scatter.6
  188.2 24.2 reduce-scatter.8
  214.2 52.1 all-gather.13
  268.4 50.3 all-gather.11
  365.2 22.3 reduce-scatter.12
  390.9 25.6 reduce-scatter.10
  419.7 25.0 reduce-scatter.14
  447.2 52.9 all-reduce.11
  531.4 27.7 reduce-scatter.16
  560.7 53.7 all-gather.15
  616.7 50.3 all-gather.17
Sparse Core Ops, SparseCore 1:
  34.0 135.5 all-reduce.9
